TPU v7x, 32 devices: a whole 2x2x4 slice. The times are simulated.
32 devices in a mesh: groups: 2 (over y), seq: 8 (over z, x), chan: 2 (over core).
Axes of the slice: x: 2, y: 2, z: 4, core: 2. Of those that a mesh axis runs over, the one named last changes fastest.
Arguments:
- signal: bfloat16 [4096, 1024], P(('groups', 'seq'), 'chan'), parts along dimension 0, may hold values from -6 to 6
- tangent: bfloat16 [4096, 1024], P(('groups', 'seq'), 'chan'), parts along dimension 0, may hold values from -6 to 6
- gains: float32 [2, 1024], P(None, 'chan'), may hold values from 0.5 to 2
- convolution_kernel: bfloat16 [2, 3072, 2, 512], P(None, 'seq', None, 'chan'), may hold values from -0.109375 to 0.109375
- mixing_kernel: bfloat16 [2, 512, 1024], P(None, 'seq', 'chan'), may hold values from -0.25 to 0.25
Outputs:
- out_signal: bfloat16 [4096, 1024], P(('groups', 'seq'), 'chan'), parts along dimension 0
- out_tangent: bfloat16 [4096, 1024], P(('groups', 'seq'), 'chan'), parts along dimension 0
There are 2 independent parts, one for each index of `groups`. A program takes and returns all parts, laid end to end along the dimension named above; an argument that names none is the same for every part. Nothing has to cross between parts.
All inputs are finite; a program needn't handle non-finite values.
Results may differ from a plain program's by a relative error of at most 0.0063.
Values may be sent and summed in bfloat16 or wider, within the bound.
No kernel may reach another device: no remote copies, remote signals or barrier semaphores. Data moves between devices by JAX's collectives and lax.ppermute only.
A program may use at most 64 MiB of HBM per device.

v0:
```python
import jax
import jax.numpy as jnp
from jax import lax
from jax.sharding import PartitionSpec as P

LAYERS = 2


def from_behind(block, axis, distance):
    devices = range(lax.axis_size(axis))
    route = [(i - distance, i) for i in devices if i - distance in devices]
    return lax.ppermute(block, axis, route)


def delayed_rows(block, delay_offset, mover):
    rows = block.shape[1]
    whole, rest = divmod(delay_offset, rows)
    parts = []
    if rest:
        parts.append(mover(block[:, rows - rest :], whole + 1))
    parts.append(mover(block[:, : rows - rest], whole))
    return jnp.concatenate(parts, 1)


def on_device(signal, tangent, gains, convolution_kernel, mixing_kernel):
    rows = signal.shape[0]
    half = signal.shape[1]
    width = half * lax.axis_size("chan")
    branch = convolution_kernel.shape[3]
    base = rows * lax.axis_size("seq") // 16
    state = signal
    dstate = tangent

    def move_half(piece, by):
        return from_behind(piece, "seq", by)

    for layer_number in range(LAYERS):
        dilation_step = base * 2**layer_number
        xval = state.astype(jnp.float32)
        dxval = dstate.astype(jnp.float32)
        partial_value = jnp.stack([jnp.sum(xval * xval, axis=1), jnp.sum(xval * dxval, axis=1)], 0)
        totals = lax.psum(partial_value, "chan")
        mean_sq = (totals[0] / width)[:, None]
        mean_cross = (totals[1] / width)[:, None]
        scale = lax.rsqrt(mean_sq + 1e-05)
        gain = gains[layer_number][None, :]
        normed = (gain * xval * scale).astype(jnp.bfloat16)
        dnormed = (gain * (dxval * scale - xval * scale * scale * scale * mean_cross)).astype(
            jnp.bfloat16
        )
        paired = jnp.stack([normed, dnormed], 0)
        taps = jnp.stack(
            [
                paired,
                delayed_rows(paired, dilation_step, move_half),
                delayed_rows(paired, 2 * dilation_step, move_half),
            ],
            2,
        )
        stacked = lax.all_gather(taps, "chan", axis=3, tiled=True)
        left = stacked.reshape(2 * rows, 3 * width)
        conv_local = convolution_kernel[layer_number].reshape(
            convolution_kernel.shape[1], 2 * branch
        )
        conv_whole = lax.all_gather(conv_local, "seq", axis=0, tiled=True)
        full = jnp.dot(left, conv_whole, preferred_element_type=jnp.float32)
        filt, gate = (full[:rows, :branch], full[:rows, branch:])
        dfilt, dgate = (full[rows:, :branch], full[rows:, branch:])
        tanh_f = jnp.tanh(filt)
        sig_g = jax.nn.sigmoid(gate)
        gated = (tanh_f * sig_g).astype(jnp.bfloat16)
        dgated = (
            (1.0 - tanh_f * tanh_f) * sig_g * dfilt + tanh_f * sig_g * (1.0 - sig_g) * dgate
        ).astype(jnp.bfloat16)
        branch_all = lax.all_gather(jnp.concatenate([gated, dgated], 0), "chan", axis=1, tiled=True)
        mix_whole = lax.all_gather(mixing_kernel[layer_number], "seq", axis=0, tiled=True)
        mixed = jnp.dot(branch_all, mix_whole, preferred_element_type=jnp.float32)
        state = (xval + mixed[:rows]).astype(jnp.bfloat16)
        dstate = (dxval + mixed[rows:]).astype(jnp.bfloat16)
    return (state, dstate)


def solution(mesh):
    return jax.shard_map(
        on_device,
        mesh=mesh,
        in_specs=(
            P(("groups", "seq"), "chan"),
            P(("groups", "seq"), "chan"),
            P(None, "chan"),
            P(None, "seq", None, "chan"),
            P(None, "seq", "chan"),
        ),
        out_specs=(P(("groups", "seq"), "chan"), P(("groups", "seq"), "chan")),
        check_vma=False,
    )
```

profile of v0, /device:TPU:0, one launch (start us, length us, event | category | flops | bytes accessed | tf_op | source)
XLA Modules:
  0.0 246.1 jit_solution(518207839076454163)
XLA Ops:
  7.2 0.0 all-gather.7.cloned.1.call-start
  7.2 1.1 copy.13
  8.3 1.1 copy.14
  9.4 0.1 fusion.10
  9.5 2.6 %psum.14 = f32[2,256]{1,0:T(2,128)S(1)} all-reduce(f32[2,256]{1,0:T(2,128)S(1)} %pad_maximum_fusion.6), channel_id=1, replica_groups=mesh['groups'=2,'seq'=8,'chan'=2] {'chan'}, use_global_device_ids=true, to_apply=%region_2.0 | all-reduce | flops 512 | bytes 4096 | tf_op jit(solution)/shard_map/psum | solution.py:42
  12.1 0.8 fusion.58
  12.9 0.2 fusion.29
  13.1 0.1 fusion.53
  13.2 4.8 %collective-permute-start.2 = (bf16[2,256,512]{1,2,0:T(8,128)(2,1)S(1)}, bf16[2,256,512]{1,2,0:T(8,128)(2,1)S(1)}, u32[]{:S(2)}, u32[]{:S(2)}) collective-permute-start(bf16[2,256,512]{1,2,0:T(8,128)(2,1)S(1)} %get-tuple-element.23), channel_id=1, source_target_pairs={{0,2},{2,4},{4,6},{6,8},{8,10},{10,12},{12,14},{1,3},{3,5},{5,7},{... | collective-permute-start | bytes 1572872 | tf_op jit(solution)/shard_map/ppermute | solution.py:12
  18.0 0.1 fusion.32
  18.1 3.6 %collective-permute-start = (bf16[2,128,512]{1,2,0:T(8,128)(2,1)S(1)}, bf16[2,128,512]{1,2,0:T(8,128)(2,1)S(1)}, u32[]{:S(2)}, u32[]{:S(2)}) collective-permute-start(bf16[2,128,512]{1,2,0:T(8,128)(2,1)S(1)} %get-tuple-element.24), channel_id=1, source_target_pairs={{0,2},{2,4},{4,6},{6,8},{8,10},{10,12},{12,14},{1,3},{3,5},{5,7},{... | collective-permute-start | bytes 786440 | tf_op jit(solution)/shard_map/ppermute | solution.py:12
  21.7 13.4 %collective-permute-done = bf16[2,128,512]{1,2,0:T(8,128)(2,1)S(1)} collective-permute-done((bf16[2,128,512]{1,2,0:T(8,128)(2,1)S(1)}, bf16[2,128,512]{1,2,0:T(8,128)(2,1)S(1)}, u32[]{:S(2)}, u32[]{:S(2)}) %collective-permute-start) | collective-permute-done | bytes 262176 | tf_op jit(solution)/shard_map/ppermute | solution.py:12
  35.1 0.1 maximum_bitcast_fusion
  35.2 1.3 pad_maximum_fusion
  36.5 0.0 all-gather.9.cloned.1.call-start
  36.6 0.5 fusion.56
  37.1 0.9 copy.23
  38.0 0.0 all-gather.11.cloned.1.call-start
  38.1 34.5 %all-gather = bf16[1,512,512]{2,1,0:T(8,128)(2,1)S(1)} all-gather(bf16[1,64,512]{2,1,0:T(8,128)(2,1)S(1)} %get-tuple-element.31), channel_id=2, replica_groups=mesh['groups'=2,'seq'=8,'chan'=2] {'seq'}, dimensions={1}, use_global_device_ids=true | all-gather | bytes 589824 | tf_op jit(solution)/shard_map/all_gather | solution.py:76
  72.6 5.1 %copy.15 = bf16[2,256,3,1024]{1,0,3,2:T(2,128)(2,1)S(1)} copy(bf16[2,256,3,1024]{1,3,0,2:T(8,128)(2,1)} %all-gather.7.cloned.1.call-done) | data formatting | bytes 6291456 | tf_op jit(solution)/shard_map/all_gather | solution.py:60
  77.7 2.2 copy.22
  79.9 35.4 %all-gather.9.cloned.1.call-done = bf16[3072,512]{1,0:T(8,128)(2,1)} async-done(((bf16[384,512]{1,0:T(8,128)(2,1)}), bf16[3072,512]{1,0:T(8,128)(2,1)}) %all-gather.9.cloned.1.call-update) | async-done | bytes 3145744 | tf_op jit(solution)/shard_map/all_gather | solution.py:65
  115.4 4.6 %fusion.59 = f32[512,512]{1,0:T(8,128)S(1)} fusion(bf16[512,3072]{0,1:T(8,128)(2,1)} %bitcast.57, bf16[3072,512]{1,0:T(8,128)(2,1)} %all-gather.9.cloned.1.call-done), kind=kOutput, calls=%fused_computation.96 | convolution fusion | flops 1610612736 | bytes 7340032 | tf_op jit(solution)/shard_map/dot_general | solution.py:66
  120.0 0.1 fusion.47
  120.2 2.2 all_gather.26
  122.4 0.5 fusion.26
  122.9 0.2 fusion.18
  123.0 2.5 %psum.15 = f32[2,256]{1,0:T(2,128)S(1)} all-reduce(f32[2,256]{1,0:T(2,128)S(1)} %pad_maximum_fusion.7), channel_id=1, replica_groups=mesh['groups'=2,'seq'=8,'chan'=2] {'chan'}, use_global_device_ids=true, to_apply=%region_5.0 | all-reduce | flops 512 | bytes 4096 | tf_op jit(solution)/shard_map/psum | solution.py:42
  125.5 0.2 fusion.28
  125.8 0.1 fusion.52
  125.8 2.5 %collective-permute-start.3 = (bf16[2,256,512]{1,2,0:T(8,128)(2,1)S(1)}, bf16[2,256,512]{1,2,0:T(8,128)(2,1)S(1)}, u32[]{:S(2)}, u32[]{:S(2)}) collective-permute-start(bf16[2,256,512]{1,2,0:T(8,128)(2,1)S(1)} %get-tuple-element.21), channel_id=1, source_target_pairs={{0,2},{2,4},{4,6},{6,8},{8,10},{10,12},{12,14},{1,3},{3,5},{5,7},{... | collective-permute-start | bytes 1572872 | tf_op jit(solution)/shard_map/ppermute | solution.py:12
  128.4 3.3 %collective-permute-start.4 = (bf16[2,256,512]{1,2,0:T(8,128)(2,1)S(1)}, bf16[2,256,512]{1,2,0:T(8,128)(2,1)S(1)}, u32[]{:S(2)}, u32[]{:S(2)}) collective-permute-start(bf16[2,256,512]{1,2,0:T(8,128)(2,1)S(1)} %get-tuple-element.21), channel_id=1, source_target_pairs={{0,4},{2,6},{4,8},{6,10},{8,12},{10,14},{1,5},{3,7},{5,9},{7,11},{... | collective-permute-start | bytes 1572872 | tf_op jit(solution)/shard_map/ppermute | solution.py:12
  131.7 8.1 %collective-permute-done.3 = bf16[2,256,512]{1,2,0:T(8,128)(2,1)S(1)} collective-permute-done((bf16[2,256,512]{1,2,0:T(8,128)(2,1)S(1)}, bf16[2,256,512]{1,2,0:T(8,128)(2,1)S(1)}, u32[]{:S(2)}, u32[]{:S(2)}) %collective-permute-start.3) | collective-permute-done | bytes 524320 | tf_op jit(solution)/shard_map/ppermute | solution.py:12
  139.8 3.1 %collective-permute-done.4 = bf16[2,256,512]{1,2,0:T(8,128)(2,1)S(1)} collective-permute-done((bf16[2,256,512]{1,2,0:T(8,128)(2,1)S(1)}, bf16[2,256,512]{1,2,0:T(8,128)(2,1)S(1)}, u32[]{:S(2)}, u32[]{:S(2)}) %collective-permute-start.4) | collective-permute-done | bytes 524320 | tf_op jit(solution)/shard_map/ppermute | solution.py:12
  142.9 1.3 pad_maximum_fusion.1
  144.2 0.0 all-gather.13.cloned.1.call-start
  144.3 0.9 copy.25
  145.2 40.1 %all-gather.1 = bf16[1,512,512]{2,1,0:T(8,128)(2,1)S(1)} all-gather(bf16[1,64,512]{2,1,0:T(8,128)(2,1)S(1)} %get-tuple-element.30), channel_id=3, replica_groups=mesh['groups'=2,'seq'=8,'chan'=2] {'seq'}, dimensions={1}, use_global_device_ids=true | all-gather | bytes 589824 | tf_op jit(solution)/shard_map/all_gather | solution.py:76
  185.3 5.1 %copy.16 = bf16[2,256,3,1024]{1,0,3,2:T(2,128)(2,1)S(1)} copy(bf16[2,256,3,1024]{1,3,0,2:T(8,128)(2,1)} %all-gather.11.cloned.1.call-done) | data formatting | bytes 6291456 | tf_op jit(solution)/shard_map/all_gather | solution.py:60
  190.4 2.2 copy.24
  192.7 37.5 %all-gather.13.cloned.1.call-done = bf16[3072,512]{1,0:T(8,128)(2,1)} async-done(((bf16[384,512]{1,0:T(8,128)(2,1)}), bf16[3072,512]{1,0:T(8,128)(2,1)}) %all-gather.13.cloned.1.call-update) | async-done | bytes 3145744 | tf_op jit(solution)/shard_map/all_gather | solution.py:65
  230.2 4.6 %fusion.60 = f32[512,512]{1,0:T(8,128)S(1)} fusion(bf16[512,3072]{0,1:T(8,128)(2,1)} %bitcast.58, bf16[3072,512]{1,0:T(8,128)(2,1)} %all-gather.13.cloned.1.call-done), kind=kOutput, calls=%fused_computation.97 | convolution fusion | flops 1610612736 | bytes 7340032 | tf_op jit(solution)/shard_map/dot_general | solution.py:66
  234.9 0.1 fusion.46
  235.1 2.2 all_gather.30
  237.2 0.5 fusion.24
  237.7 0.1 fusion.7
  237.8 0.8 copy.19
  238.7 0.8 copy.20
  (20 shorter events, 0.2 us)
Async XLA Ops:
  7.2 65.4 %all-gather.7.cloned.1.call-start = ((), (), s32[]{:S(2)}) async-start(), calls=%async_computation | async-start | bytes 4718592 | tf_op jit(solution)/shard_map/all_gather | solution.py:60
  13.2 21.9 %collective-permute-start.2 = (bf16[2,256,512]{1,2,0:T(8,128)(2,1)S(1)}, bf16[2,256,512]{1,2,0:T(8,128)(2,1)S(1)}, u32[]{:S(2)}, u32[]{:S(2)}) collective-permute-start(bf16[2,256,512]{1,2,0:T(8,128)(2,1)S(1)} %get-tuple-element.23), channel_id=1, source_target_pairs={{0,2},{2,4},{4,6},{6,8},{8,10},{10,12},{12,14},{1,3},{3,5},{5,7},{... | collective-permute-start | bytes 1572872 | tf_op jit(solution)/shard_map/ppermute | solution.py:12
  18.1 18.5 %copy-start = (bf16[2,384,2,256]{3,2,1,0:T(2,128)(2,1)S(1)}, bf16[2,384,2,256]{3,2,1,0:T(2,128)(2,1)}, u32[]{:S(2)}) copy-start(bf16[2,384,2,256]{3,2,1,0:T(2,128)(2,1)} %param.8) | copy-start | bytes 2359300
  18.1 17.0 %collective-permute-start = (bf16[2,128,512]{1,2,0:T(8,128)(2,1)S(1)}, bf16[2,128,512]{1,2,0:T(8,128)(2,1)S(1)}, u32[]{:S(2)}, u32[]{:S(2)}) collective-permute-start(bf16[2,128,512]{1,2,0:T(8,128)(2,1)S(1)} %get-tuple-element.24), channel_id=1, source_target_pairs={{0,2},{2,4},{4,6},{6,8},{8,10},{10,12},{12,14},{1,3},{3,5},{5,7},{... | collective-permute-start | bytes 786440 | tf_op jit(solution)/shard_map/ppermute | solution.py:12
  21.6 13.4 %collective-permute-start.1 = (bf16[2,128,512]{1,2,0:T(8,128)(2,1)S(1)}, bf16[2,128,512]{1,2,0:T(8,128)(2,1)S(1)}, u32[]{:S(2)}, u32[]{:S(2)}) collective-permute-start(bf16[2,128,512]{1,2,0:T(8,128)(2,1)S(1)} %get-tuple-element.25), channel_id=1, source_target_pairs={{0,0},{2,2},{4,4},{6,6},{8,8},{10,10},{12,12},{14,14},{1,1},{3,3},... | collective-permute-start | bytes 786440 | tf_op jit(solution)/shard_map/ppermute | solution.py:12
  35.1 2.9 %copy-start.1 = (bf16[2,64,512]{2,1,0:T(8,128)(2,1)S(1)}, bf16[2,64,512]{2,1,0:T(8,128)(2,1)}, u32[]{:S(2)}) copy-start(bf16[2,64,512]{2,1,0:T(8,128)(2,1)} %param.9) | copy-start | bytes 393220
  36.5 78.9 %all-gather.9.cloned.1.call-start = ((), (), s32[]{:S(2)}) async-start(), calls=%async_computation.1 | async-start | bytes 3538944 | tf_op jit(solution)/shard_map/all_gather | solution.py:65
  38.0 147.3 %all-gather.11.cloned.1.call-start = ((), (), s32[]{:S(2)}) async-start(), calls=%async_computation.2 | async-start | bytes 4718592 | tf_op jit(solution)/shard_map/all_gather | solution.py:60
  125.8 14.0 %collective-permute-start.3 = (bf16[2,256,512]{1,2,0:T(8,128)(2,1)S(1)}, bf16[2,256,512]{1,2,0:T(8,128)(2,1)S(1)}, u32[]{:S(2)}, u32[]{:S(2)}) collective-permute-start(bf16[2,256,512]{1,2,0:T(8,128)(2,1)S(1)} %get-tuple-element.21), channel_id=1, source_target_pairs={{0,2},{2,4},{4,6},{6,8},{8,10},{10,12},{12,14},{1,3},{3,5},{5,7},{... | collective-permute-start | bytes 1572872 | tf_op jit(solution)/shard_map/ppermute | solution.py:12
  128.4 14.5 %collective-permute-start.4 = (bf16[2,256,512]{1,2,0:T(8,128)(2,1)S(1)}, bf16[2,256,512]{1,2,0:T(8,128)(2,1)S(1)}, u32[]{:S(2)}, u32[]{:S(2)}) collective-permute-start(bf16[2,256,512]{1,2,0:T(8,128)(2,1)S(1)} %get-tuple-element.21), channel_id=1, source_target_pairs={{0,4},{2,6},{4,8},{6,10},{8,12},{10,14},{1,5},{3,7},{5,9},{7,11},{... | collective-permute-start | bytes 1572872 | tf_op jit(solution)/shard_map/ppermute | solution.py:12
  144.2 86.0 %all-gather.13.cloned.1.call-start = ((), (), s32[]{:S(2)}) async-start(), calls=%async_computation.3 | async-start | bytes 3538944 | tf_op jit(solution)/shard_map/all_gather | solution.py:65
Sparse Core Ops, SparseCore 0:
  36.6 14.3 all-gather.6
  53.2 62.1 all-gather.8
  144.4 21.7 all-gather.10
  168.2 62.0 all-gather.12
where the time goes:
time: 247 us; the launch traced here: 246 us
  waiting for transfers between devices  97.6 us (40%)
  blocking collectives  84 us (34%)
  local copies, waits for them, and re-layouts  21.7 us (9%)
  starting transfers between devices  14.4 us (6%)
  between operations  14 us (6%)
  matrix products  10.3 us (4%)
  other arithmetic  4.16 us (2%)
    all_gather x2, blocking collectives, on_device(): lax.all_gather(mixing_kernel[layer_number], 'seq', axis=0, tiled=True)  74.6 us
    all_gather x2, waiting for transfers between devices, on_device(): conv_whole = lax.all_gather(conv_local, 'seq', axis=0, tiled=True)  73 us
    ppermute x5, waiting for transfers between devices, from_behind(): return lax.ppermute(block, axis, route)  24.6 us
    ppermute x5, starting transfers between devices, from_behind(): return lax.ppermute(block, axis, route)  14.2 us
    all_gather x2, local copies, waits for them, and re-layouts, on_device(): stacked = lax.all_gather(taps, 'chan', axis=3, tiled=True)  10.3 us
    unnamed x12, local copies, waits for them, and re-layouts  10.1 us
    dot_general x2, matrix products, on_device(): full = jnp.dot(left, conv_whole, preferred_element_type=jnp.float32)  9.3 us
    psum x2, blocking collectives, on_device(): totals = lax.psum(partial_value, 'chan')  5.06 us
  transfers between devices with their start and end apart: 9, of which 5 were waited for; matrix products, arithmetic and copies ran while one was open for 7% of the time, Pallas kernels for 0%

commit v1 on v0

--- a/solution.py
+++ b/solution.py
@@ -39,7 +39,7 @@
         xval = state.astype(jnp.float32)
         dxval = dstate.astype(jnp.float32)
         partial_value = jnp.stack([jnp.sum(xval * xval, axis=1), jnp.sum(xval * dxval, axis=1)], 0)
-        totals = lax.psum(partial_value, "chan")
+        totals = jnp.sum(lax.all_gather(partial_value, "chan"), axis=0)
         mean_sq = (totals[0] / width)[:, None]
         mean_cross = (totals[1] / width)[:, None]
         scale = lax.rsqrt(mean_sq + 1e-05)

time: 247 us -> 245 us (level)
    psum x2 -> x0, blocking collectives: 5.06 us -> none  [on_device(): totals = lax.psum(partial_value, 'chan')]
    all_gather x0 -> x2, blocking collectives: none -> 3.71 us  [on_device(): totals = jnp.sum(lax.all_gather(partial_value, 'chan'), axis=0)]
    all_gather x2, blocking collectives: 74.6 us -> 77.1 us  [on_device(): lax.all_gather(mixing_kernel[layer_number], 'seq', axis=0, tiled=True)]
    unnamed x12 -> x18, local copies, waits for them, and re-layouts: 10.1 us -> 8.5 us
  transfers between devices with their start and end apart: 9 -> 9, of which waited for: 5 -> 5; matrix products, arithmetic and copies ran while one was open for 7% -> 6% of each run, Pallas kernels for 0% -> 0%
where the time goes in v1:
time: 245 us; the launch traced here: 244 us
  waiting for transfers between devices  96.9 us (40%)
  blocking collectives  85.2 us (35%)
  local copies, waits for them, and re-layouts  20.1 us (8%)
  starting transfers between devices  14.3 us (6%)
  between operations  14 us (6%)
  matrix products  9.37 us (4%)
  other arithmetic  4.19 us (2%)
    all_gather x2, blocking collectives, on_device(): lax.all_gather(mixing_kernel[layer_number], 'seq', axis=0, tiled=True)  77.1 us
    all_gather x2, waiting for transfers between devices, on_device(): conv_whole = lax.all_gather(conv_local, 'seq', axis=0, tiled=True)  72.2 us
    ppermute x5, waiting for transfers between devices, from_behind(): return lax.ppermute(block, axis, route)  24.7 us
    ppermute x5, starting transfers between devices, from_behind(): return lax.ppermute(block, axis, route)  14.2 us
    all_gather x2, local copies, waits for them, and re-layouts, on_device(): stacked = lax.all_gather(taps, 'chan', axis=3, tiled=True)  10.3 us
    unnamed x18, local copies, waits for them, and re-layouts  8.5 us
    dot_general x2, matrix products, on_device(): full = jnp.dot(left, conv_whole, preferred_element_type=jnp.float32)  8.4 us
  transfers between devices with their start and end apart: 9, of which 5 were waited for; matrix products, arithmetic and copies ran while one was open for 6% of the time, Pallas kernels for 0%

profile of v1, /device:TPU:0, one launch (start us, length us, event | category | flops | bytes accessed | tf_op | source)
XLA Modules:
  0.0 244.1 jit_solution(14915733902010601634)
XLA Ops:
  7.2 0.0 all-gather.11.cloned.1.call-start
  7.2 1.1 copy.21
  8.3 1.1 copy.22
  9.4 0.1 fusion.10
  9.5 1.9 all-gather.4
  11.5 0.8 fusion.58
  12.3 0.2 fusion.29
  12.5 0.1 fusion.53
  12.6 4.7 %collective-permute-start.2 = (bf16[2,256,512]{1,2,0:T(8,128)(2,1)S(1)}, bf16[2,256,512]{1,2,0:T(8,128)(2,1)S(1)}, u32[]{:S(2)}, u32[]{:S(2)}) collective-permute-start(bf16[2,256,512]{1,2,0:T(8,128)(2,1)S(1)} %get-tuple-element.25), channel_id=1, source_target_pairs={{0,2},{2,4},{4,6},{6,8},{8,10},{10,12},{12,14},{1,3},{3,5},{5,7},{... | collective-permute-start | bytes 1572872 | tf_op jit(solution)/shard_map/ppermute | solution.py:12
  17.3 0.1 fusion.32
  17.4 3.6 %collective-permute-start = (bf16[2,128,512]{1,2,0:T(8,128)(2,1)S(1)}, bf16[2,128,512]{1,2,0:T(8,128)(2,1)S(1)}, u32[]{:S(2)}, u32[]{:S(2)}) collective-permute-start(bf16[2,128,512]{1,2,0:T(8,128)(2,1)S(1)} %get-tuple-element.26), channel_id=1, source_target_pairs={{0,2},{2,4},{4,6},{6,8},{8,10},{10,12},{12,14},{1,3},{3,5},{5,7},{... | collective-permute-start | bytes 786440 | tf_op jit(solution)/shard_map/ppermute | solution.py:12
  21.0 13.4 %collective-permute-done = bf16[2,128,512]{1,2,0:T(8,128)(2,1)S(1)} collective-permute-done((bf16[2,128,512]{1,2,0:T(8,128)(2,1)S(1)}, bf16[2,128,512]{1,2,0:T(8,128)(2,1)S(1)}, u32[]{:S(2)}, u32[]{:S(2)}) %collective-permute-start) | collective-permute-done | bytes 262176 | tf_op jit(solution)/shard_map/ppermute | solution.py:12
  34.4 0.1 maximum_bitcast_fusion
  34.5 1.3 pad_maximum_fusion
  35.9 0.0 all-gather.13.cloned.1.call-start
  35.9 0.5 fusion.56
  36.5 0.9 copy.31
  37.4 0.0 all-gather.15.cloned.1.call-start
  37.4 34.5 %all-gather.1 = bf16[1,512,512]{2,1,0:T(8,128)(2,1)S(1)} all-gather(bf16[1,64,512]{2,1,0:T(8,128)(2,1)S(1)} %get-tuple-element.33), channel_id=3, replica_groups=mesh['groups'=2,'seq'=8,'chan'=2] {'seq'}, dimensions={1}, use_global_device_ids=true | all-gather | bytes 589824 | tf_op jit(solution)/shard_map/all_gather | solution.py:76
  71.9 5.1 %copy.23 = bf16[2,256,3,1024]{1,0,3,2:T(2,128)(2,1)S(1)} copy(bf16[2,256,3,1024]{1,3,0,2:T(8,128)(2,1)} %all-gather.11.cloned.1.call-done) | data formatting | bytes 6291456 | tf_op jit(solution)/shard_map/all_gather | solution.py:60
  77.1 2.3 copy.30
  79.3 35.4 %all-gather.13.cloned.1.call-done = bf16[3072,512]{1,0:T(8,128)(2,1)} async-done(((bf16[384,512]{1,0:T(8,128)(2,1)}), bf16[3072,512]{1,0:T(8,128)(2,1)}) %all-gather.13.cloned.1.call-update) | async-done | bytes 3145744 | tf_op jit(solution)/shard_map/all_gather | solution.py:65
  114.7 4.6 %fusion.59 = f32[512,512]{1,0:T(8,128)S(1)} fusion(bf16[512,3072]{0,1:T(8,128)(2,1)} %bitcast.61, bf16[3072,512]{1,0:T(8,128)(2,1)} %all-gather.13.cloned.1.call-done), kind=kOutput, calls=%fused_computation.96 | convolution fusion | flops 1610612736 | bytes 7340032 | tf_op jit(solution)/shard_map/dot_general | solution.py:66
  119.4 0.1 fusion.47
  119.6 2.2 all_gather.40
  121.7 0.5 fusion.26
  122.2 0.2 fusion.18
  122.4 1.8 all-gather.5
  124.2 0.2 fusion.28
  124.5 0.1 fusion.52
  124.6 2.5 %collective-permute-start.3 = (bf16[2,256,512]{1,2,0:T(8,128)(2,1)S(1)}, bf16[2,256,512]{1,2,0:T(8,128)(2,1)S(1)}, u32[]{:S(2)}, u32[]{:S(2)}) collective-permute-start(bf16[2,256,512]{1,2,0:T(8,128)(2,1)S(1)} %get-tuple-element.23), channel_id=1, source_target_pairs={{0,2},{2,4},{4,6},{6,8},{8,10},{10,12},{12,14},{1,3},{3,5},{5,7},{... | collective-permute-start | bytes 1572872 | tf_op jit(solution)/shard_map/ppermute | solution.py:12
  127.1 3.4 %collective-permute-start.4 = (bf16[2,256,512]{1,2,0:T(8,128)(2,1)S(1)}, bf16[2,256,512]{1,2,0:T(8,128)(2,1)S(1)}, u32[]{:S(2)}, u32[]{:S(2)}) collective-permute-start(bf16[2,256,512]{1,2,0:T(8,128)(2,1)S(1)} %get-tuple-element.23), channel_id=1, source_target_pairs={{0,4},{2,6},{4,8},{6,10},{8,12},{10,14},{1,5},{3,7},{5,9},{7,11},{... | collective-permute-start | bytes 1572872 | tf_op jit(solution)/shard_map/ppermute | solution.py:12
  130.4 8.1 %collective-permute-done.3 = bf16[2,256,512]{1,2,0:T(8,128)(2,1)S(1)} collective-permute-done((bf16[2,256,512]{1,2,0:T(8,128)(2,1)S(1)}, bf16[2,256,512]{1,2,0:T(8,128)(2,1)S(1)}, u32[]{:S(2)}, u32[]{:S(2)}) %collective-permute-start.3) | collective-permute-done | bytes 524320 | tf_op jit(solution)/shard_map/ppermute | solution.py:12
  138.6 3.1 %collective-permute-done.4 = bf16[2,256,512]{1,2,0:T(8,128)(2,1)S(1)} collective-permute-done((bf16[2,256,512]{1,2,0:T(8,128)(2,1)S(1)}, bf16[2,256,512]{1,2,0:T(8,128)(2,1)S(1)}, u32[]{:S(2)}, u32[]{:S(2)}) %collective-permute-start.4) | collective-permute-done | bytes 524320 | tf_op jit(solution)/shard_map/ppermute | solution.py:12
  141.6 1.3 pad_maximum_fusion.1
  143.0 0.0 all-gather.17.cloned.1.call-start
  143.0 0.8 copy.33
  143.9 42.6 %all-gather.3 = bf16[1,512,512]{2,1,0:T(8,128)(2,1)} all-gather(bf16[1,64,512]{2,1,0:T(8,128)(2,1)S(1)} %get-tuple-element.32), channel_id=5, replica_groups=mesh['groups'=2,'seq'=8,'chan'=2] {'seq'}, dimensions={1}, use_global_device_ids=true | all-gather | bytes 589824 | tf_op jit(solution)/shard_map/all_gather | solution.py:76
  186.5 5.1 %copy.24 = bf16[2,256,3,1024]{1,0,3,2:T(2,128)(2,1)S(1)} copy(bf16[2,256,3,1024]{1,3,0,2:T(8,128)(2,1)} %all-gather.15.cloned.1.call-done) | data formatting | bytes 6291456 | tf_op jit(solution)/shard_map/all_gather | solution.py:60
  191.7 0.7 copy.32
  192.3 36.8 %all-gather.17.cloned.1.call-done = bf16[3072,512]{1,0:T(8,128)(2,1)} async-done(((bf16[384,512]{1,0:T(8,128)(2,1)}), bf16[3072,512]{1,0:T(8,128)(2,1)}) %all-gather.17.cloned.1.call-update) | async-done | bytes 3145744 | tf_op jit(solution)/shard_map/all_gather | solution.py:65
  229.2 3.8 %fusion.60 = f32[512,512]{1,0:T(8,128)S(1)} fusion(bf16[512,3072]{0,1:T(8,128)(2,1)S(1)} %bitcast.62, bf16[3072,512]{1,0:T(8,128)(2,1)} %all-gather.17.cloned.1.call-done), kind=kOutput, calls=%fused_computation.97 | convolution fusion | flops 1610612736 | bytes 7340032 | tf_op jit(solution)/shard_map/dot_general | solution.py:66
  232.9 0.1 fusion.46
  233.1 2.2 all_gather.46
  235.3 0.5 fusion.24
  235.8 0.1 fusion.7
  235.9 0.8 copy.27
  236.8 0.8 copy.28
  (28 shorter events, 0.2 us)
Async XLA Ops:
  7.2 64.8 %all-gather.11.cloned.1.call-start = ((), (), s32[]{:S(2)}) async-start(), calls=%async_computation | async-start | bytes 4718592 | tf_op jit(solution)/shard_map/all_gather | solution.py:60
  12.6 21.9 %collective-permute-start.2 = (bf16[2,256,512]{1,2,0:T(8,128)(2,1)S(1)}, bf16[2,256,512]{1,2,0:T(8,128)(2,1)S(1)}, u32[]{:S(2)}, u32[]{:S(2)}) collective-permute-start(bf16[2,256,512]{1,2,0:T(8,128)(2,1)S(1)} %get-tuple-element.25), channel_id=1, source_target_pairs={{0,2},{2,4},{4,6},{6,8},{8,10},{10,12},{12,14},{1,3},{3,5},{5,7},{... | collective-permute-start | bytes 1572872 | tf_op jit(solution)/shard_map/ppermute | solution.py:12
  17.4 18.5 %copy-start.3 = (bf16[2,384,2,256]{3,2,1,0:T(2,128)(2,1)S(1)}, bf16[2,384,2,256]{3,2,1,0:T(2,128)(2,1)}, u32[]{:S(2)}) copy-start(bf16[2,384,2,256]{3,2,1,0:T(2,128)(2,1)} %param.8) | copy-start | bytes 2359300
  17.4 17.0 %collective-permute-start = (bf16[2,128,512]{1,2,0:T(8,128)(2,1)S(1)}, bf16[2,128,512]{1,2,0:T(8,128)(2,1)S(1)}, u32[]{:S(2)}, u32[]{:S(2)}) collective-permute-start(bf16[2,128,512]{1,2,0:T(8,128)(2,1)S(1)} %get-tuple-element.26), channel_id=1, source_target_pairs={{0,2},{2,4},{4,6},{6,8},{8,10},{10,12},{12,14},{1,3},{3,5},{5,7},{... | collective-permute-start | bytes 786440 | tf_op jit(solution)/shard_map/ppermute | solution.py:12
  21.0 13.5 %collective-permute-start.1 = (bf16[2,128,512]{1,2,0:T(8,128)(2,1)S(1)}, bf16[2,128,512]{1,2,0:T(8,128)(2,1)S(1)}, u32[]{:S(2)}, u32[]{:S(2)}) collective-permute-start(bf16[2,128,512]{1,2,0:T(8,128)(2,1)S(1)} %get-tuple-element.27), channel_id=1, source_target_pairs={{0,0},{2,2},{4,4},{6,6},{8,8},{10,10},{12,12},{14,14},{1,1},{3,3},... | collective-permute-start | bytes 786440 | tf_op jit(solution)/shard_map/ppermute | solution.py:12
  34.5 2.9 %copy-start.4 = (bf16[2,64,512]{2,1,0:T(8,128)(2,1)S(1)}, bf16[2,64,512]{2,1,0:T(8,128)(2,1)}, u32[]{:S(2)}) copy-start(bf16[2,64,512]{2,1,0:T(8,128)(2,1)} %param.9) | copy-start | bytes 393220
  35.9 78.9 %all-gather.13.cloned.1.call-start = ((), (), s32[]{:S(2)}) async-start(), calls=%async_computation.1 | async-start | bytes 3538944 | tf_op jit(solution)/shard_map/all_gather | solution.py:65
  37.4 149.2 %all-gather.15.cloned.1.call-start = ((), (), s32[]{:S(2)}) async-start(), calls=%async_computation.2 | async-start | bytes 4718592 | tf_op jit(solution)/shard_map/all_gather | solution.py:60
  122.4 20.6 %copy-start = (bf16[256,512]{0,1:T(8,128)(2,1)}, bf16[256,512]{0,1:T(8,128)(2,1)S(1)}, u32[]{:S(2)}) copy-start(bf16[256,512]{0,1:T(8,128)(2,1)S(1)} %get-tuple-element.13) | copy-start | bytes 786436
  124.6 14.0 %collective-permute-start.3 = (bf16[2,256,512]{1,2,0:T(8,128)(2,1)S(1)}, bf16[2,256,512]{1,2,0:T(8,128)(2,1)S(1)}, u32[]{:S(2)}, u32[]{:S(2)}) collective-permute-start(bf16[2,256,512]{1,2,0:T(8,128)(2,1)S(1)} %get-tuple-element.23), channel_id=1, source_target_pairs={{0,2},{2,4},{4,6},{6,8},{8,10},{10,12},{12,14},{1,3},{3,5},{5,7},{... | collective-permute-start | bytes 1572872 | tf_op jit(solution)/shard_map/ppermute | solution.py:12
  127.1 14.6 %collective-permute-start.4 = (bf16[2,256,512]{1,2,0:T(8,128)(2,1)S(1)}, bf16[2,256,512]{1,2,0:T(8,128)(2,1)S(1)}, u32[]{:S(2)}, u32[]{:S(2)}) collective-permute-start(bf16[2,256,512]{1,2,0:T(8,128)(2,1)S(1)} %get-tuple-element.23), channel_id=1, source_target_pairs={{0,4},{2,6},{4,8},{6,10},{8,12},{10,14},{1,5},{3,7},{5,9},{7,11},{... | collective-permute-start | bytes 1572872 | tf_op jit(solution)/shard_map/ppermute | solution.py:12
  143.0 86.2 %all-gather.17.cloned.1.call-start = ((), (), s32[]{:S(2)}) async-start(), calls=%async_computation.3 | async-start | bytes 3538944 | tf_op jit(solution)/shard_map/all_gather | solution.py:65
  229.1 6.1 %copy-start.2 = (bf16[1,512,512]{2,1,0:T(8,128)(2,1)S(1)}, bf16[1,512,512]{2,1,0:T(8,128)(2,1)}, u32[]{:S(2)}) copy-start(bf16[1,512,512]{2,1,0:T(8,128)(2,1)} %all-gather.3) | copy-start | bytes 1572868
  232.9 2.9 %copy-start.1 = (bf16[256,512]{0,1:T(8,128)(2,1)S(1)}, bf16[256,512]{0,1:T(8,128)(2,1)}, u32[]{:S(2)}) copy-start(bf16[256,512]{0,1:T(8,128)(2,1)} %copy-done) | copy-start | bytes 786436
Sparse Core Ops, SparseCore 0:
  36.0 14.3 all-gather.10
  52.6 62.1 all-gather.12
  143.1 21.7 all-gather.14
  166.9 62.1 all-gather.16
